TPU v7x, 128 devices: a whole 4x4x4 slice. The times are simulated.
128 devices in a mesh: req: 4 (over x), tp: 32 (over z, y, core).
Axes of the slice: x: 4, y: 4, z: 4, core: 2. Of those that a mesh axis runs over, the one named last changes fastest.
Arguments:
- step_inputs: bfloat16 [4, 256, 1536], P(None, ('req', 'tp')), may hold values from -6 to 6
- qkv_weight: bfloat16 [1536, 2048], replicated, may hold values from -0.15625 to 0.15625
- qkv_bias: float32 [2048], replicated, may hold values from -8 to 8
- out_weight: bfloat16 [1536, 1536], P('tp'), may hold values from -0.15625 to 0.15625
- gate_weight: bfloat16 [1536, 8960], P(None, 'tp'), may hold values from -0.15625 to 0.15625
- up_weight: bfloat16 [1536, 8960], P(None, 'tp'), may hold values from -0.15625 to 0.15625
- down_weight: bfloat16 [8960, 1536], P('tp'), may hold values from -0.0625 to 0.0625
- cache_keys: bfloat16 [256, 4096, 256], P(('req', 'tp')), may hold values from -60 to 60
- cache_values: bfloat16 [256, 4096, 256], P(('req', 'tp')), may hold values from -24 to 24
- lengths: int32 [32, 8], replicated, may hold values from 1 to 4096, as said below
- parents: int32 [4, 32, 8], replicated, may hold values from 0 to 7
- slot_request: int32 [32], replicated, may hold values from 0 to 31, each once
Outputs:
- outputs: bfloat16 [4, 256, 1536], P(None, ('req', 'tp'))
Inputs may be any that keep to these rules, and one draw needn't show every extreme that they name: lengths[r, c] is the number of cached positions of beam c of request r; some beam has exactly 4096. parents[t, r, b] names a beam of the same request r. `slot_request`: a permutation of the requests; slots 8 * i to 8 * i + 7 are rows of index i of req.
All inputs are finite; a program needn't handle non-finite values.
Results may differ from a plain program's by a relative error of at most 0.022.
The roundings to bfloat16 on the way count: a program that leaves them out, or rounds other values in their place, can miss the bound.
Values may be sent and summed in bfloat16 or wider, within the bound.
No kernel may reach another device: no remote copies, remote signals or barrier semaphores. Data moves between devices by JAX's collectives and lax.ppermute only.
A program may use at most 128 MiB of HBM per device.

v0:
```python
import jax
import jax.numpy as jnp
from jax import lax
from jax.sharding import PartitionSpec as P

Q_HEADS = 12
KV_HEADS = 2
theta_base = 1000000.0
norm_eps = 1e-06
masked_score = -1e30


def rms_normed(values):
    values = values.astype(jnp.float32)
    factor = lax.rsqrt(jnp.mean(values * values, axis=-1, keepdims=True) + norm_eps)
    return (values * factor).astype(jnp.bfloat16)


def rotate(vectors, positions):
    half = vectors.shape[-1] // 2
    freqs = theta_base ** (-jnp.arange(half, dtype=jnp.float32) * 2.0 / vectors.shape[-1])
    angles = positions.astype(jnp.float32)[:, None] * freqs[None, :]
    cosine = jnp.cos(angles)[:, None, :]
    sine = jnp.sin(angles)[:, None, :]
    values = vectors.astype(jnp.float32)
    first = values[..., :half]
    second = values[..., half:]
    return jnp.concatenate(
        [first * cosine - second * sine, second * cosine + first * sine], axis=-1
    ).astype(jnp.bfloat16)


def owner_rows(flat, owned_count, beams, inverse):
    owned_global = flat * owned_count + jnp.arange(owned_count, dtype=jnp.int32)
    owned_request = owned_global // beams
    owned_beam = owned_global % beams
    beam_range = jnp.arange(beams, dtype=jnp.int32)
    query_rows = (inverse[owned_request][:, None] * beams + beam_range[None, :]).reshape(-1)
    return (owned_request, owned_beam, query_rows)


def owned_attention(
    every_query, keys, values, owned_request, owned_beam, query_rows, root_all, lengths
):
    owned_rows, context, kv_width = keys.shape
    beams = root_all.shape[1]
    head_dim = kv_width // KV_HEADS
    group = Q_HEADS // KV_HEADS
    grouped = jnp.take(every_query, query_rows, axis=0).reshape(
        owned_rows, beams, KV_HEADS, group, head_dim
    )
    keys = keys.reshape(owned_rows, context, KV_HEADS, head_dim)
    values = values.reshape(owned_rows, context, KV_HEADS, head_dim)
    scores = jnp.einsum(
        "jbkgd,jpkd->jbkgp", grouped, keys, preferred_element_type=jnp.float32
    ) * head_dim ** (-0.5)
    limits = lengths[owned_request, owned_beam]
    live = (jnp.arange(context, dtype=jnp.int32)[None, :] < limits[:, None])[:, None, None, None, :]
    scores = jnp.where(live, scores, masked_score)
    peak = jnp.max(scores, axis=-1)
    weights = jnp.where(live, jnp.exp(scores - peak[..., None]), 0.0)
    total = jnp.sum(weights, axis=-1)
    output = jnp.einsum(
        "jbkgp,jpkd->jbkgd",
        weights.astype(jnp.bfloat16),
        values,
        preferred_element_type=jnp.float32,
    )
    chosen = (root_all[owned_request] == owned_beam[:, None])[:, :, None, None]
    peak = jnp.where(chosen, peak, 0.0).reshape(owned_rows * beams, KV_HEADS, group)
    total = jnp.where(chosen, total, 0.0).reshape(owned_rows * beams, KV_HEADS, group)
    output = jnp.where(chosen[..., None], output, 0.0).reshape(
        owned_rows * beams, KV_HEADS, group, head_dim
    )
    return (peak, total, output)


def spread_rows(pieces, target_rows, row_count):
    return tuple(
        (
            jnp.zeros((row_count,) + piece.shape[1:], jnp.float32).at[target_rows].add(piece)
            for piece in pieces
        )
    )


def per_device(
    step_inputs,
    qkv_weight,
    qkv_bias,
    out_weight,
    gate_weight,
    up_weight,
    down_weight,
    cache_keys,
    cache_values,
    lengths,
    parents,
    slot_request,
):
    steps_count, rows_dev, width = step_inputs.shape
    beams = parents.shape[2]
    requests = slot_request.shape[0]
    req_count = lax.axis_size("req")
    tp_count = lax.axis_size("tp")
    group_requests = requests // req_count
    group_rows = group_requests * beams
    total_rows = requests * beams
    owned_count = cache_keys.shape[0]
    kv_width = cache_keys.shape[2]
    head_dim = kv_width // KV_HEADS
    group = Q_HEADS // KV_HEADS
    attn_width = Q_HEADS * head_dim
    req_index = lax.axis_index("req")
    tp_index = lax.axis_index("tp")
    flat_index = req_index * tp_count + tp_index
    my_requests = lax.dynamic_slice_in_dim(slot_request, req_index * group_requests, group_requests)
    inverse = (
        jnp.zeros((requests,), jnp.int32)
        .at[slot_request]
        .set(jnp.arange(requests, dtype=jnp.int32))
    )
    owned_request, owned_beam, query_rows = owner_rows(flat_index, owned_count, beams, inverse)
    beam_range = jnp.arange(beams, dtype=jnp.int32)
    root_all = jnp.broadcast_to(beam_range[None, :], (requests, beams))
    gen_keys = jnp.zeros((steps_count, group_rows, kv_width), jnp.bfloat16)
    gen_values = jnp.zeros((steps_count, group_rows, kv_width), jnp.bfloat16)
    base_rows = (jnp.arange(group_requests, dtype=jnp.int32) * beams)[:, None]
    column_width = out_weight.shape[0]
    results = []
    for step in range(steps_count):
        root_all = jnp.take_along_axis(root_all, parents[step], axis=1)
        reorder = (base_rows + parents[step][my_requests]).reshape(-1)
        gen_keys = jnp.take(gen_keys, reorder, axis=1)
        gen_values = jnp.take(gen_values, reorder, axis=1)
        inputs = step_inputs[step]
        normed = rms_normed(inputs)
        qkv = (
            jnp.dot(
                lax.all_gather(normed, "tp", axis=0, tiled=True),
                qkv_weight,
                preferred_element_type=jnp.float32,
            )
            + qkv_bias
        ).astype(jnp.bfloat16)
        my_roots = root_all[my_requests]
        positions = (jnp.take_along_axis(lengths[my_requests], my_roots, axis=1) + step).reshape(-1)
        queries = rotate(qkv[:, :attn_width].reshape(group_rows, Q_HEADS, head_dim), positions)
        new_keys = rotate(
            qkv[:, attn_width : attn_width + kv_width].reshape(group_rows, KV_HEADS, head_dim),
            positions,
        )
        gen_keys = gen_keys.at[step].set(new_keys.reshape(group_rows, kv_width))
        gen_values = gen_values.at[step].set(qkv[:, attn_width + kv_width :])
        every_query = lax.all_gather(
            queries.reshape(group_rows, attn_width), "req", axis=0, tiled=True
        )
        part_peak, part_total, part_output = owned_attention(
            every_query,
            cache_keys,
            cache_values,
            owned_request,
            owned_beam,
            query_rows,
            root_all,
            lengths,
        )
        all_peak, all_total, all_output = spread_rows(
            (part_peak, part_total, part_output), query_rows, total_rows
        )
        sum_peak, sum_total, sum_output = lax.psum((all_peak, all_total, all_output), ("req", "tp"))
        peak = lax.dynamic_slice_in_dim(sum_peak, req_index * group_rows, group_rows, 0)
        total = lax.dynamic_slice_in_dim(sum_total, req_index * group_rows, group_rows, 0)
        output = lax.dynamic_slice_in_dim(sum_output, req_index * group_rows, group_rows, 0)
        grouped = queries.reshape(group_rows, KV_HEADS, group, head_dim)
        past_keys = gen_keys[: step + 1].reshape(step + 1, group_rows, KV_HEADS, head_dim)
        past_values = gen_values[: step + 1].reshape(step + 1, group_rows, KV_HEADS, head_dim)
        recent_scores = jnp.einsum(
            "bkgd,sbkd->bkgs", grouped, past_keys, preferred_element_type=jnp.float32
        ) * head_dim ** (-0.5)
        top = jnp.maximum(peak, jnp.max(recent_scores, axis=-1))
        factor = jnp.exp(peak - top)
        recent_weights = jnp.exp(recent_scores - top[..., None])
        denominator = total * factor + jnp.sum(recent_weights, axis=-1)
        numerator = output * factor[..., None] + jnp.einsum(
            "bkgs,sbkd->bkgd",
            recent_weights.astype(jnp.bfloat16),
            past_values,
            preferred_element_type=jnp.float32,
        )
        attention = (
            (numerator / denominator[..., None])
            .reshape(group_rows, attn_width)
            .astype(jnp.bfloat16)
        )
        columns = lax.dynamic_slice_in_dim(attention, tp_index * column_width, column_width, 1)
        attended = lax.psum_scatter(
            jnp.dot(columns, out_weight, preferred_element_type=jnp.float32).astype(jnp.bfloat16),
            "tp",
            scatter_dimension=0,
            tiled=True,
        ).astype(jnp.float32)
        middle = inputs.astype(jnp.float32) + attended
        mixed_in = rms_normed(middle)
        piece = lax.all_gather(mixed_in, "tp", axis=0, tiled=True)
        gate = jnp.dot(piece, gate_weight, preferred_element_type=jnp.float32)
        upward = jnp.dot(piece, up_weight, preferred_element_type=jnp.float32)
        hidden = (jax.nn.silu(gate) * upward).astype(jnp.bfloat16)
        lowered = lax.psum_scatter(
            jnp.dot(hidden, down_weight, preferred_element_type=jnp.float32).astype(jnp.bfloat16),
            "tp",
            scatter_dimension=0,
            tiled=True,
        ).astype(jnp.float32)
        results.append((middle + lowered).astype(jnp.bfloat16))
    return jnp.stack(results)


def solution(mesh):
    in_specs = (
        P(None, ("req", "tp"), None),
        P(),
        P(),
        P("tp", None),
        P(None, "tp"),
        P(None, "tp"),
        P("tp", None),
        P(("req", "tp"), None, None),
        P(("req", "tp"), None, None),
        P(),
        P(),
        P(),
    )
    out_specs = P(None, ("req", "tp"), None)
    return jax.shard_map(
        per_device, mesh=mesh, in_specs=in_specs, out_specs=out_specs, check_vma=False
    )
```

profile of v0, /device:TPU:1, one launch (start us, length us, event | category | flops | bytes accessed | tf_op | source)
XLA Modules:
  0.0 1172.3 jit_solution(9988134711650191990)
XLA Ops:
  28.1 27.6 %all-gather = bf16[32,2,1536]{2,1,0:T(2,128)(2,1)S(1)} all-gather(bf16[1,2,1536]{2,1,0:T(2,128)(2,1)S(1)} %fusion.170), channel_id=1, replica_groups=mesh['req'=4,'tp'=32] {'tp'}, dimensions={0}, use_global_device_ids=true | all-gather | bytes 202752 | tf_op jit(solution)/shard_map/all_gather | solution.py:140
  55.8 4.0 fusion.28
  61.5 12.0 %all_gather.37 = bf16[256,1536]{1,0:T(8,128)(2,1)S(1)} all-gather(bf16[64,1536]{1,0:T(8,128)(2,1)S(1)} %bitcast.314), channel_id=1, replica_groups=mesh['req'=4,'tp'=32] {'req'}, dimensions={0}, use_global_device_ids=true | all-gather | bytes 983040 | tf_op jit(solution)/shard_map/all_gather | solution.py:155
  74.2 7.0 reshape.1079
  81.2 6.9 reshape.1080
  108.8 67.0 %all-reduce.9 = (f32[256,2,6]{0,1,2:T(2,128)S(1)}, f32[256,2,6]{0,1,2:T(2,128)S(1)}) all-reduce(f32[256,2,6]{0,1,2:T(2,128)S(1)} %copy.328, f32[256,2,6]{0,1,2:T(2,128)S(1)} %copy.335), channel_id=1, replica_groups=mesh['req'=4,'tp'=32] {'req','tp'}, use_global_device_ids=true, to_apply=%region_6.10 | all-reduce | flops 6144 | bytes 49152 | tf_op jit(solution)/shard_map/psum | solution.py:171
  185.9 63.2 %all-reduce.20.cloned.1.call-done = f32[256,2,6,128]{3,1,2,0:T(2,128)} async-done(((f32[256,2,6,128]{3,1,2,0:T(2,128)}), f32[256,2,6,128]{3,1,2,0:T(2,128)}) %all-reduce.20.cloned.1.call-update) | async-done | bytes 1572880 | tf_op jit(solution)/shard_map/psum | solution.py:171
  253.4 98.8 %all-reduce.22.cloned.1.call-done = bf16[64,1536]{1,0:T(8,128)(2,1)} async-done(((bf16[64,1536]{1,0:T(8,128)(2,1)}), bf16[64,1536]{1,0:T(8,128)(2,1)}) %all-reduce.22.cloned.1.call-update) | async-done | bytes 196624
  354.6 24.5 %all-gather.4 = bf16[32,2,1536]{2,1,0:T(2,128)(2,1)S(1)} all-gather(bf16[1,2,1536]{2,1,0:T(2,128)(2,1)S(1)} %get-tuple-element.172), channel_id=1, replica_groups=mesh['req'=4,'tp'=32] {'tp'}, dimensions={0}, use_global_device_ids=true | all-gather | bytes 202752 | tf_op jit(solution)/shard_map/all_gather | solution.py:140
  383.8 23.3 %all-gather.2 = bf16[32,2,1536]{2,1,0:T(2,128)(2,1)S(1)} all-gather(bf16[1,2,1536]{2,1,0:T(2,128)(2,1)S(1)} %get-tuple-element.171), channel_id=1, replica_groups=mesh['req'=4,'tp'=32] {'tp'}, dimensions={0}, use_global_device_ids=true | all-gather | bytes 202752 | tf_op jit(solution)/shard_map/all_gather | solution.py:140
  407.2 4.0 fusion.29
  414.6 23.7 %all-gather.6 = bf16[32,2,1536]{2,1,0:T(2,128)(2,1)S(1)} all-gather(bf16[1,2,1536]{2,1,0:T(2,128)(2,1)S(1)} %get-tuple-element.173), channel_id=1, replica_groups=mesh['req'=4,'tp'=32] {'tp'}, dimensions={0}, use_global_device_ids=true | all-gather | bytes 202752 | tf_op jit(solution)/shard_map/all_gather | solution.py:140
  438.5 4.0 fusion.31
  443.4 11.9 %all_gather.46 = bf16[256,1536]{1,0:T(8,128)(2,1)S(1)} all-gather(bf16[64,1536]{1,0:T(8,128)(2,1)S(1)} %bitcast.315), channel_id=1, replica_groups=mesh['req'=4,'tp'=32] {'req'}, dimensions={0}, use_global_device_ids=true | all-gather | bytes 983040 | tf_op jit(solution)/shard_map/all_gather | solution.py:155
  458.1 10.9 all_gather.40
  470.6 11.8 %all_gather.43 = bf16[256,1536]{1,0:T(8,128)(2,1)S(1)} all-gather(bf16[64,1536]{1,0:T(8,128)(2,1)S(1)} %bitcast.317), channel_id=1, replica_groups=mesh['req'=4,'tp'=32] {'req'}, dimensions={0}, use_global_device_ids=true | all-gather | bytes 983040 | tf_op jit(solution)/shard_map/all_gather | solution.py:155
  551.3 30.5 %all-gather.1 = bf16[32,2,1536]{2,1,0:T(2,128)(2,1)S(1)} all-gather(bf16[1,2,1536]{2,1,0:T(2,128)(2,1)S(1)} %copy-done.66), channel_id=1, replica_groups=mesh['req'=4,'tp'=32] {'tp'}, dimensions={0}, use_global_device_ids=true | all-gather | bytes 202752 | tf_op jit(solution)/shard_map/all_gather | solution.py:205
  588.9 119.1 %all-reduce.24.cloned.1.call-done = (f32[256,2,6]{2,1,0:T(2,128)}, f32[256,2,6]{2,1,0:T(2,128)}, f32[256,2,6]{2,1,0:T(2,128)}, f32[256,2,6]{2,1,0:T(2,128)}, f32[256,2,6]{2,1,0:T(2,128)}, /*index=5*/f32[256,2,6]{2,1,0:T(2,128)}) async-done(((f32[256,2,6]{2,1,0:T(2,128)}, f32[256,2,6]{2,1,0:T(2,128)}, f32[256,2,6]{2,1,0:T(2,128)}, f32[256,2,6]{2,1,0:T(2,128)}, f32[256,2,6]{2,1,0:T(2,128)}, ...) | async-done | bytes 73744 | tf_op jit(solution)/shard_map/psum | solution.py:171
  715.0 154.8 %all-reduce.26.cloned.1.call-done = (f32[256,2,6,128]{3,2,1,0:T(8,128)}, f32[256,2,6,128]{3,2,1,0:T(8,128)}, f32[256,2,6,128]{3,2,1,0:T(8,128)}) async-done(((f32[256,2,6,128]{3,2,1,0:T(8,128)}, f32[256,2,6,128]{3,2,1,0:T(8,128)}, f32[256,2,6,128]{3,2,1,0:T(8,128)}), (f32[256,2,6,128]{3,2,1,0:T(8,128)}, f32[256,2,6,128]{3,2,1,0:T(8,128)}, f32[256,2,6,128]{3,2,1,0:T(8,128)})) %all-reduce.26.cloned.1.call-update) | async-done | bytes 4718608 | tf_op jit(solution)/shard_map/psum | solution.py:171
  880.4 100.5 %all-reduce.30.cloned.1.call-done = (bf16[64,1536]{1,0:T(8,128)(2,1)}, bf16[64,1536]{1,0:T(8,128)(2,1)}, bf16[64,1536]{1,0:T(8,128)(2,1)}) async-done(((bf16[64,1536]{1,0:T(8,128)(2,1)}, bf16[64,1536]{1,0:T(8,128)(2,1)}, bf16[64,1536]{1,0:T(8,128)(2,1)}), (bf16[64,1536]{1,0:T(8,128)(2,1)}, bf16[64,1536]{1,0:T(8,128)(2,1)}, bf16[64,1536]{1,0:T(8,128)(2,1)})) %all-reduce.30.cloned.1.call-update) | async-done | bytes 589840
  982.8 24.9 %all-gather.3 = bf16[32,2,1536]{2,1,0:T(2,128)(2,1)S(1)} all-gather(bf16[1,2,1536]{2,1,0:T(2,128)(2,1)S(1)} %get-tuple-element.174), channel_id=1, replica_groups=mesh['req'=4,'tp'=32] {'tp'}, dimensions={0}, use_global_device_ids=true | all-gather | bytes 202752 | tf_op jit(solution)/shard_map/all_gather | solution.py:205
  1009.9 22.5 %all-gather.5 = bf16[32,2,1536]{2,1,0:T(2,128)(2,1)S(1)} all-gather(bf16[1,2,1536]{2,1,0:T(2,128)(2,1)S(1)} %get-tuple-element.176), channel_id=1, replica_groups=mesh['req'=4,'tp'=32] {'tp'}, dimensions={0}, use_global_device_ids=true | all-gather | bytes 202752 | tf_op jit(solution)/shard_map/all_gather | solution.py:205
  1034.5 24.1 %all-gather.7 = bf16[32,2,1536]{2,1,0:T(2,128)(2,1)S(1)} all-gather(bf16[1,2,1536]{2,1,0:T(2,128)(2,1)S(1)} %get-tuple-element.175), channel_id=1, replica_groups=mesh['req'=4,'tp'=32] {'tp'}, dimensions={0}, use_global_device_ids=true | all-gather | bytes 202752 | tf_op jit(solution)/shard_map/all_gather | solution.py:205
  1060.8 102.6 %all-reduce.28.cloned.1.call-done = (bf16[64,1536]{1,0:T(8,128)(2,1)}, bf16[64,1536]{1,0:T(8,128)(2,1)}, bf16[64,1536]{1,0:T(8,128)(2,1)}, bf16[64,1536]{1,0:T(8,128)(2,1)}) async-done(((bf16[64,1536]{1,0:T(8,128)(2,1)}, bf16[64,1536]{1,0:T(8,128)(2,1)}, bf16[64,1536]{1,0:T(8,128)(2,1)}, bf16[64,1536]{1,0:T(8,128)(2,1)}), (bf16[64,1536]{1,0:T(8,128)(2,1)}, bf16[64,1536]{1,0:T(8,128)(2,1)}, ...) | async-done | bytes 786448
  (502 shorter events, 176.0 us)
Async XLA Ops:
  6.5 872.2 %copy-start = (bf16[280,1536]{1,0:T(8,128)(2,1)S(1)}, bf16[280,1536]{1,0:T(8,128)(2,1)}, u32[]{:S(2)}) copy-start(bf16[280,1536]{1,0:T(8,128)(2,1)} %param.42) | copy-start | bytes 2580484
  6.5 242.6 %all-reduce.20.cloned.1.call-start = ((), (), s32[]{:S(2)}) async-start(), calls=%async_computation | async-start | bytes 3145728 | tf_op jit(solution)/shard_map/psum | solution.py:171
  8.8 79.9 %copy-start.68 = (pred[16]{0:T(512)(128)(4,1)}, pred[16]{0:T(512)(128)(4,1)S(1)}, u32[]{:S(2)}) copy-start(pred[16]{0:T(512)(128)(4,1)S(1)} %compare_and_fusion.4) | copy-start | bytes 52
  26.7 29.1 %copy-start.53 = (f32[2048]{0:T(1024)S(1)}, f32[2048]{0:T(1024)}, u32[]{:S(2)}) copy-start(f32[2048]{0:T(1024)} %param.38) | copy-start | bytes 24580
  61.0 20.2 %copy-start.42 = (f32[64,64]{1,0:T(8,128)}, f32[64,64]{1,0:T(8,128)S(1)}, u32[]{:S(2)}) copy-start(f32[64,64]{1,0:T(8,128)S(1)} %get-tuple-element.217) | copy-start | bytes 49156
  61.0 20.2 %copy-start.44 = (f32[64,64]{1,0:T(8,128)}, f32[64,64]{1,0:T(8,128)S(1)}, u32[]{:S(2)}) copy-start(f32[64,64]{1,0:T(8,128)S(1)} %get-tuple-element.218) | copy-start | bytes 49156
  98.5 253.7 %all-reduce.22.cloned.1.call-start = ((), (), s32[]{:S(2)}) async-start(), calls=%async_computation.1 | async-start | bytes 393216
  102.3 78.6 %copy-start.75 = (pred[2,8]{1,0:T(4,128)(4,1)S(1)}, pred[2,8]{1,0:T(4,128)(4,1)}, u32[]{:S(2)}) copy-start(pred[2,8]{1,0:T(4,128)(4,1)} %get-tuple-element.206) | copy-start | bytes 52
  102.3 79.1 %copy-start.73 = (pred[2,8]{1,0:T(4,128)(4,1)S(1)}, pred[2,8]{1,0:T(4,128)(4,1)}, u32[]{:S(2)}) copy-start(pred[2,8]{1,0:T(4,128)(4,1)} %get-tuple-element.208) | copy-start | bytes 52
  102.3 79.7 %copy-start.71 = (pred[2,8]{1,0:T(4,128)(4,1)S(1)}, pred[2,8]{1,0:T(4,128)(4,1)}, u32[]{:S(2)}) copy-start(pred[2,8]{1,0:T(4,128)(4,1)} %get-tuple-element.207) | copy-start | bytes 52
  102.3 80.3 %copy-start.79 = (u32[128]{0:T(128)S(1)}, u32[128]{0:T(128)}, u32[]{:S(2)}) copy-start(u32[128]{0:T(128)} %constant.501) | copy-start | bytes 1540
  107.5 144.8 %copy-start.9 = (bf16[48,1536]{1,0:T(8,128)(2,1)S(1)}, bf16[48,1536]{1,0:T(8,128)(2,1)}, u32[]{:S(2)}) copy-start(bf16[48,1536]{1,0:T(8,128)(2,1)} %param.39) | copy-start | bytes 442372
  253.3 454.6 %all-reduce.24.cloned.1.call-start = ((), (), s32[]{:S(2)}) async-start(), calls=%async_computation.2 | async-start | bytes 3145728 | tf_op jit(solution)/shard_map/psum | solution.py:171
  456.8 26.4 %copy-start.69 = (pred[16]{0:T(512)(128)(4,1)S(1)}, pred[16]{0:T(512)(128)(4,1)}, u32[]{:S(2)}) copy-start(pred[16]{0:T(512)(128)(4,1)} %copy-done.68) | copy-start | bytes 52
  499.4 17.5 %copy-start.55 = (bf16[1,64,256]{2,1,0:T(8,128)(2,1)S(1)}, bf16[1,64,256]{2,1,0:T(8,128)(2,1)}, u32[]{:S(2)}) copy-start(bf16[1,64,256]{2,1,0:T(8,128)(2,1)} %get-tuple-element.151) | copy-start | bytes 98308
  529.2 16.5 %copy-start.62 = (f32[16,2,6]{2,1,0:T(2,128)S(1)}, f32[16,2,6]{2,1,0:T(2,128)}, u32[]{:S(2)}) copy-start(f32[16,2,6]{2,1,0:T(2,128)} %copy.387) | copy-start | bytes 2308
  529.2 17.7 %copy-start.65 = (f32[16,2,6]{2,1,0:T(2,128)S(1)}, f32[16,2,6]{2,1,0:T(2,128)}, u32[]{:S(2)}) copy-start(f32[16,2,6]{2,1,0:T(2,128)} %copy.359) | copy-start | bytes 2308
  529.2 18.9 %copy-start.64 = (f32[16,2,6]{2,1,0:T(2,128)S(1)}, f32[16,2,6]{2,1,0:T(2,128)}, u32[]{:S(2)}) copy-start(f32[16,2,6]{2,1,0:T(2,128)} %copy.345) | copy-start | bytes 2308
  537.9 44.0 %copy-start.52 = (bf16[1,64,256]{2,0,1:T(2,128)(2,1)S(1)}, bf16[1,64,256]{2,0,1:T(2,128)(2,1)}, u32[]{:S(2)}) copy-start(bf16[1,64,256]{2,0,1:T(2,128)(2,1)} %copy.395) | copy-start | bytes 98308
  551.3 318.5 %all-reduce.26.cloned.1.call-start = ((), (), s32[]{:S(2)}) async-start(), calls=%async_computation.3 | async-start | bytes 12582912 | tf_op jit(solution)/shard_map/psum | solution.py:171
  585.8 284.0 %copy-start.29 = (bf16[4,64,256]{2,0,1:T(4,128)(2,1)S(1)}, bf16[4,64,256]{2,0,1:T(4,128)(2,1)}, u32[]{:S(2)}) copy-start(bf16[4,64,256]{2,0,1:T(4,128)(2,1)} %copy-done.28) | copy-start | bytes 393220
  585.8 395.1 %all-reduce.30.cloned.1.call-start = ((), (), s32[]{:S(2)}) async-start(), calls=%async_computation.5 | async-start | bytes 1179648
  587.9 283.4 %copy-start.57 = (f32[64,2,6,2]{2,3,1,0:T(2,128)}, f32[64,2,6,2]{2,3,1,0:T(2,128)S(1)}, u32[]{:S(2)}) copy-start(f32[64,2,6,2]{2,3,1,0:T(2,128)S(1)} %get-tuple-element.230) | copy-start | bytes 18436
  878.3 285.2 %all-reduce.28.cloned.1.call-start = ((), (), s32[]{:S(2)}) async-start(), calls=%async_computation.4 | async-start | bytes 1572864
  (62 other events, 354.3 us)
Sparse Core Ops, SparseCore 0:
  98.6 150.4 all-reduce.19
  253.5 98.6 all-reduce.21
  551.4 156.4 all-reduce.23
  713.0 156.7 all-reduce.25
  878.4 102.5 all-reduce.29
  1060.9 102.4 all-reduce.27
where the time goes:
time: 1180 us; the launch traced here: 1170 us
  waiting for transfers between devices  639 us (54%)
  blocking collectives  315 us (27%)
  local copies, waits for them, and re-layouts  95.5 us (8%)
  other arithmetic  53.3 us (5%)
  matrix products  52.6 us (4%)
  between operations  16.6 us (1%)
    psum x3, waiting for transfers between devices, per_device(): lax.psum((all_peak, all_total, all_output), ('req', 'tp'))  337 us
    unnamed x9, waiting for transfers between devices  302 us
    all_gather x4, blocking collectives, per_device(): piece = lax.all_gather(mixed_in, 'tp', axis=0, tiled=True)  102 us
    all_gather x4, blocking collectives, per_device(): lax.all_gather(normed, 'tp', axis=0, tiled=True)  99.2 us
    psum x1, blocking collectives, per_device(): lax.psum((all_peak, all_total, all_output), ('req', 'tp'))  67 us
    all_gather x4, blocking collectives, per_device(): lax.all_gather(queries.reshape(group_rows, attn_width), 'req', axis=0, ti...  46.6 us
  transfers between devices with their start and end apart: 6, of which 6 were waited for; matrix products, arithmetic and copies ran while one was open for 3% of the time, Pallas kernels for 0%

commit v1 on v0

--- a/solution.py
+++ b/solution.py
@@ -8,6 +8,12 @@
 theta_base = 1000000.0
 norm_eps = 1e-06
 masked_score = -1e30
+
+
+def joined_along(blocks, dim):
+    blocks = jnp.moveaxis(blocks, 0, dim)
+    lengths = blocks.shape
+    return blocks.reshape(*lengths[:dim], lengths[dim] * lengths[dim + 1], *lengths[dim + 2 :])
 
 
 def rms_normed(values):
@@ -152,9 +158,20 @@
         )
         gen_keys = gen_keys.at[step].set(new_keys.reshape(group_rows, kv_width))
         gen_values = gen_values.at[step].set(qkv[:, attn_width + kv_width :])
-        every_query = lax.all_gather(
-            queries.reshape(group_rows, attn_width), "req", axis=0, tiled=True
-        )
+        x = queries.reshape(group_rows, attn_width)
+        size = lax.axis_size("req")
+        pairs = [(i, (i + 1) % size) for i in range(size)]
+        back = [(b, a) for a, b in pairs]
+        lower, upper = ([], [])
+        for k in range(size - 1):
+            if k % 2 == 0:
+                lower.append(lax.ppermute(lower[-1] if lower else x, "req", pairs))
+            else:
+                upper.append(lax.ppermute(upper[-1] if upper else x, "req", back))
+        tiles = jnp.stack([*lower[::-1], x, *upper])
+        shift = lax.axis_index("req") - len(lower)
+        tiles = tiles[(jnp.arange(size) - shift) % size]
+        every_query = joined_along(tiles, 0)
         part_peak, part_total, part_output = owned_attention(
             every_query,
             cache_keys,

time: 1180 us -> 1170 us (level)
  blocking collectives: 315 us -> 260 us
  waiting for transfers between devices: 639 us -> 672 us
  starting transfers between devices: 0.42 us -> 13 us
    all_gather x4 -> x0, blocking collectives: 46.6 us -> none  [per_device(): lax.all_gather(queries.reshape(group_rows, attn_width), 'req', axis=0, ti...]
    psum x3, waiting for transfers between devices: 337 us -> 358 us  [per_device(): lax.psum((all_peak, all_total, all_output), ('req', 'tp'))]
    ppermute x0 -> x12, waiting for transfers between devices: none -> 12.6 us  [the longest x8 12.6 us: per_device(): lower.append(lax.ppermute(lower[-1] if lower else x, 'req', pairs))]
    ppermute x0 -> x12, starting transfers between devices: none -> 12.5 us  [the longest x4 8.42 us: per_device(): upper.append(lax.ppermute(upper[-1] if upper else x, 'req', back))]
  transfers between devices with their start and end apart: 6 -> 18, of which waited for: 6 -> 10; matrix products, arithmetic and copies ran while one was open for 3% -> 9% of each run, Pallas kernels for 0% -> 0%
where the time goes in v1:
time: 1170 us; the launch traced here: 1160 us
  waiting for transfers between devices  672 us (57%)
  blocking collectives  260 us (22%)
  local copies, waits for them, and re-layouts  90 us (8%)
  other arithmetic  54.4 us (5%)
  matrix products  53.7 us (5%)
  between operations  16.6 us (1%)
  starting transfers between devices  13 us (1%)
    psum x3, waiting for transfers between devices, per_device(): lax.psum((all_peak, all_total, all_output), ('req', 'tp'))  358 us
    unnamed x9, waiting for transfers between devices  301 us
    all_gather x4, blocking collectives, per_device(): lax.all_gather(normed, 'tp', axis=0, tiled=True)  99.7 us
    all_gather x4, blocking collectives, per_device(): piece = lax.all_gather(mixed_in, 'tp', axis=0, tiled=True)  95 us
    psum x1, blocking collectives, per_device(): lax.psum((all_peak, all_total, all_output), ('req', 'tp'))  64.9 us
  transfers between devices with their start and end apart: 18, of which 10 were waited for; matrix products, arithmetic and copies ran while one was open for 9% of the time, Pallas kernels for 0%

profile of v1, /device:TPU:1, one launch (start us, length us, event | category | flops | bytes accessed | tf_op | source)
XLA Modules:
  0.0 1159.3 jit_solution(16566262783576145224)
XLA Ops:
  23.6 27.6 %all-gather = bf16[32,2,1536]{2,1,0:T(2,128)(2,1)S(1)} all-gather(bf16[1,2,1536]{2,1,0:T(2,128)(2,1)S(1)} %fusion.170), channel_id=1, replica_groups=mesh['req'=4,'tp'=32] {'tp'}, dimensions={0}, use_global_device_ids=true | all-gather | bytes 202752 | tf_op jit(solution)/shard_map/all_gather | solution.py:146
  51.3 4.0 fusion.28
  68.7 7.0 reshape.1185
  75.7 6.9 reshape.1186
  89.1 6.9 collective-permute-done.1
  115.9 64.9 %all-reduce.9 = (f32[256,2,6]{0,1,2:T(2,128)S(1)}, f32[256,2,6]{0,1,2:T(2,128)S(1)}) all-reduce(f32[256,2,6]{0,1,2:T(2,128)S(1)} %copy.328, f32[256,2,6]{0,1,2:T(2,128)S(1)} %copy.335), channel_id=1, replica_groups=mesh['req'=4,'tp'=32] {'req','tp'}, use_global_device_ids=true, to_apply=%region_6.10 | all-reduce | flops 6144 | bytes 49152 | tf_op jit(solution)/shard_map/psum | solution.py:188
  181.5 72.3 %all-reduce.20.cloned.1.call-done = f32[256,2,6,128]{3,1,2,0:T(2,128)} async-done(((f32[256,2,6,128]{3,1,2,0:T(2,128)}), f32[256,2,6,128]{3,1,2,0:T(2,128)}) %all-reduce.20.cloned.1.call-update) | async-done | bytes 1572880 | tf_op jit(solution)/shard_map/psum | solution.py:188
  258.7 98.2 %all-reduce.22.cloned.1.call-done = bf16[64,1536]{1,0:T(8,128)(2,1)} async-done(((bf16[64,1536]{1,0:T(8,128)(2,1)}), bf16[64,1536]{1,0:T(8,128)(2,1)}) %all-reduce.22.cloned.1.call-update) | async-done | bytes 196624
  359.2 24.5 %all-gather.4 = bf16[32,2,1536]{2,1,0:T(2,128)(2,1)S(1)} all-gather(bf16[1,2,1536]{2,1,0:T(2,128)(2,1)S(1)} %get-tuple-element.172), channel_id=1, replica_groups=mesh['req'=4,'tp'=32] {'tp'}, dimensions={0}, use_global_device_ids=true | all-gather | bytes 202752 | tf_op jit(solution)/shard_map/all_gather | solution.py:146
  383.8 4.0 fusion.30
  388.5 23.3 %all-gather.6 = bf16[32,2,1536]{2,1,0:T(2,128)(2,1)S(1)} all-gather(bf16[1,2,1536]{2,1,0:T(2,128)(2,1)S(1)} %get-tuple-element.173), channel_id=1, replica_groups=mesh['req'=4,'tp'=32] {'tp'}, dimensions={0}, use_global_device_ids=true | all-gather | bytes 202752 | tf_op jit(solution)/shard_map/all_gather | solution.py:146
  411.9 4.0 fusion.31
  420.7 24.3 %all-gather.2 = bf16[32,2,1536]{2,1,0:T(2,128)(2,1)S(1)} all-gather(bf16[1,2,1536]{2,1,0:T(2,128)(2,1)S(1)} %get-tuple-element.171), channel_id=1, replica_groups=mesh['req'=4,'tp'=32] {'tp'}, dimensions={0}, use_global_device_ids=true | all-gather | bytes 202752 | tf_op jit(solution)/shard_map/all_gather | solution.py:146
  445.1 4.0 fusion.29
  480.8 23.5 %all-gather.1 = bf16[32,2,1536]{2,1,0:T(2,128)(2,1)S(1)} all-gather(bf16[1,2,1536]{2,1,0:T(2,128)(2,1)S(1)} %copy-done.47), channel_id=1, replica_groups=mesh['req'=4,'tp'=32] {'tp'}, dimensions={0}, use_global_device_ids=true | all-gather | bytes 202752 | tf_op jit(solution)/shard_map/all_gather | solution.py:222
  524.6 4.0 fusion.208
  546.6 4.1 fusion.73
  564.1 130.8 %all-reduce.24.cloned.1.call-done = (f32[256,2,6]{2,1,0:T(2,128)}, f32[256,2,6]{2,1,0:T(2,128)}, f32[256,2,6]{2,1,0:T(2,128)}, f32[256,2,6]{2,1,0:T(2,128)}, f32[256,2,6]{2,1,0:T(2,128)}, /*index=5*/f32[256,2,6]{2,1,0:T(2,128)}) async-done(((f32[256,2,6]{2,1,0:T(2,128)}, f32[256,2,6]{2,1,0:T(2,128)}, f32[256,2,6]{2,1,0:T(2,128)}, f32[256,2,6]{2,1,0:T(2,128)}, f32[256,2,6]{2,1,0:T(2,128)}, ...) | async-done | bytes 73744 | tf_op jit(solution)/shard_map/psum | solution.py:188
  701.9 154.8 %all-reduce.26.cloned.1.call-done = (f32[256,2,6,128]{3,2,1,0:T(8,128)}, f32[256,2,6,128]{3,2,1,0:T(8,128)}, f32[256,2,6,128]{3,2,1,0:T(8,128)}) async-done(((f32[256,2,6,128]{3,2,1,0:T(8,128)}, f32[256,2,6,128]{3,2,1,0:T(8,128)}, f32[256,2,6,128]{3,2,1,0:T(8,128)}), (f32[256,2,6,128]{3,2,1,0:T(8,128)}, f32[256,2,6,128]{3,2,1,0:T(8,128)}, f32[256,2,6,128]{3,2,1,0:T(8,128)})) %all-reduce.26.cloned.1.call-update) | async-done | bytes 4718608 | tf_op jit(solution)/shard_map/psum | solution.py:188
  867.4 100.5 %all-reduce.30.cloned.1.call-done = (bf16[64,1536]{1,0:T(8,128)(2,1)}, bf16[64,1536]{1,0:T(8,128)(2,1)}, bf16[64,1536]{1,0:T(8,128)(2,1)}) async-done(((bf16[64,1536]{1,0:T(8,128)(2,1)}, bf16[64,1536]{1,0:T(8,128)(2,1)}, bf16[64,1536]{1,0:T(8,128)(2,1)}), (bf16[64,1536]{1,0:T(8,128)(2,1)}, bf16[64,1536]{1,0:T(8,128)(2,1)}, bf16[64,1536]{1,0:T(8,128)(2,1)})) %all-reduce.30.cloned.1.call-update) | async-done | bytes 589840
  969.8 24.9 %all-gather.3 = bf16[32,2,1536]{2,1,0:T(2,128)(2,1)S(1)} all-gather(bf16[1,2,1536]{2,1,0:T(2,128)(2,1)S(1)} %get-tuple-element.174), channel_id=1, replica_groups=mesh['req'=4,'tp'=32] {'tp'}, dimensions={0}, use_global_device_ids=true | all-gather | bytes 202752 | tf_op jit(solution)/shard_map/all_gather | solution.py:222
  996.8 22.5 %all-gather.5 = bf16[32,2,1536]{2,1,0:T(2,128)(2,1)S(1)} all-gather(bf16[1,2,1536]{2,1,0:T(2,128)(2,1)S(1)} %get-tuple-element.176), channel_id=1, replica_groups=mesh['req'=4,'tp'=32] {'tp'}, dimensions={0}, use_global_device_ids=true | all-gather | bytes 202752 | tf_op jit(solution)/shard_map/all_gather | solution.py:222
  1021.5 24.1 %all-gather.7 = bf16[32,2,1536]{2,1,0:T(2,128)(2,1)S(1)} all-gather(bf16[1,2,1536]{2,1,0:T(2,128)(2,1)S(1)} %get-tuple-element.175), channel_id=1, replica_groups=mesh['req'=4,'tp'=32] {'tp'}, dimensions={0}, use_global_device_ids=true | all-gather | bytes 202752 | tf_op jit(solution)/shard_map/all_gather | solution.py:222
  1047.8 102.6 %all-reduce.28.cloned.1.call-done = (bf16[64,1536]{1,0:T(8,128)(2,1)}, bf16[64,1536]{1,0:T(8,128)(2,1)}, bf16[64,1536]{1,0:T(8,128)(2,1)}, bf16[64,1536]{1,0:T(8,128)(2,1)}) async-done(((bf16[64,1536]{1,0:T(8,128)(2,1)}, bf16[64,1536]{1,0:T(8,128)(2,1)}, bf16[64,1536]{1,0:T(8,128)(2,1)}, bf16[64,1536]{1,0:T(8,128)(2,1)}), (bf16[64,1536]{1,0:T(8,128)(2,1)}, bf16[64,1536]{1,0:T(8,128)(2,1)}, ...) | async-done | bytes 786448
  (504 shorter events, 178.9 us)
Async XLA Ops:
  6.5 859.2 %copy-start = (bf16[280,1536]{1,0:T(8,128)(2,1)S(1)}, bf16[280,1536]{1,0:T(8,128)(2,1)}, u32[]{:S(2)}) copy-start(bf16[280,1536]{1,0:T(8,128)(2,1)} %param.42) | copy-start | bytes 2580484
  6.5 247.2 %all-reduce.20.cloned.1.call-start = ((), (), s32[]{:S(2)}) async-start(), calls=%async_computation | async-start | bytes 3145728 | tf_op jit(solution)/shard_map/psum | solution.py:188
  56.3 398.3 %copy-start.33 = (f32[64,64]{1,0:T(8,128)}, f32[64,64]{1,0:T(8,128)S(1)}, u32[]{:S(2)}) copy-start(f32[64,64]{1,0:T(8,128)S(1)} %get-tuple-element.182) | copy-start | bytes 49156
  56.3 398.4 %copy-start.34 = (f32[64,64]{1,0:T(8,128)}, f32[64,64]{1,0:T(8,128)S(1)}, u32[]{:S(2)}) copy-start(f32[64,64]{1,0:T(8,128)S(1)} %get-tuple-element.183) | copy-start | bytes 49156
  56.8 32.1 %collective-permute-start = (bf16[64,1536]{1,0:T(8,128)(2,1)S(1)}, bf16[64,1536]{1,0:T(8,128)(2,1)S(1)}, u32[]{:S(2)}, u32[]{:S(2)}) collective-permute-start(bf16[64,1536]{1,0:T(8,128)(2,1)S(1)} %bitcast.350), channel_id=1, source_target_pairs={{0,32},{32,64},{64,96},{96,0},{1,33},{33,65},{65,97},{97,1},{2,34}... | collective-permute-start | bytes 589832 | tf_op jit(solution)/shard_map/ppermute | solution.py:168
  58.0 31.1 %collective-permute-start.2 = (bf16[64,1536]{1,0:T(8,128)(2,1)S(1)}, bf16[64,1536]{1,0:T(8,128)(2,1)S(1)}, u32[]{:S(2)}, u32[]{:S(2)}) collective-permute-start(bf16[64,1536]{1,0:T(8,128)(2,1)S(1)} %bitcast.351), channel_id=1, source_target_pairs={{32,0},{64,32},{96,64},{0,96},{33,1},{65,33},{97,65},{1,97},{34,2}... | collective-permute-start | bytes 589832 | tf_op jit(solution)/shard_map/ppermute | solution.py:170
  88.8 7.2 collective-permute-start.1
  106.2 250.6 %all-reduce.22.cloned.1.call-start = ((), (), s32[]{:S(2)}) async-start(), calls=%async_computation.1 | async-start | bytes 393216
  110.2 146.8 %copy-start.10 = (bf16[48,1536]{1,0:T(8,128)(2,1)S(1)}, bf16[48,1536]{1,0:T(8,128)(2,1)}, u32[]{:S(2)}) copy-start(bf16[48,1536]{1,0:T(8,128)(2,1)} %param.39) | copy-start | bytes 442372
  258.0 436.9 %all-reduce.24.cloned.1.call-start = ((), (), s32[]{:S(2)}) async-start(), calls=%async_computation.2 | async-start | bytes 3145728 | tf_op jit(solution)/shard_map/psum | solution.py:188
  417.1 87.2 %collective-permute-start.9 = (bf16[64,1536]{1,0:T(8,128)(2,1)}, bf16[64,1536]{1,0:T(8,128)(2,1)}, u32[]{:S(2)}, u32[]{:S(2)}) collective-permute-start(bf16[64,1536]{1,0:T(8,128)(2,1)} %bitcast.304), channel_id=1, source_target_pairs={{0,32},{32,64},{64,96},{96,0},{1,33},{33,65},{65,97},{97,1},{2,34}... | collective-permute-start | bytes 589832 | tf_op jit(solution)/shard_map/ppermute | solution.py:168
  418.3 89.0 %collective-permute-start.11 = (bf16[64,1536]{1,0:T(8,128)(2,1)}, bf16[64,1536]{1,0:T(8,128)(2,1)}, u32[]{:S(2)}, u32[]{:S(2)}) collective-permute-start(bf16[64,1536]{1,0:T(8,128)(2,1)} %bitcast.304), channel_id=1, source_target_pairs={{32,0},{64,32},{96,64},{0,96},{33,1},{65,33},{97,65},{1,97},{34,2}... | collective-permute-start | bytes 589832 | tf_op jit(solution)/shard_map/ppermute | solution.py:170
  451.0 59.1 %collective-permute-start.3 = (bf16[64,1536]{1,0:T(8,128)(2,1)}, bf16[64,1536]{1,0:T(8,128)(2,1)}, u32[]{:S(2)}, u32[]{:S(2)}) collective-permute-start(bf16[64,1536]{1,0:T(8,128)(2,1)} %bitcast.306), channel_id=1, source_target_pairs={{0,32},{32,64},{64,96},{96,0},{1,33},{33,65},{65,97},{97,1},{2,34}... | collective-permute-start | bytes 589832 | tf_op jit(solution)/shard_map/ppermute | solution.py:168
  451.0 64.2 %collective-permute-start.5 = (bf16[64,1536]{1,0:T(8,128)(2,1)}, bf16[64,1536]{1,0:T(8,128)(2,1)}, u32[]{:S(2)}, u32[]{:S(2)}) collective-permute-start(bf16[64,1536]{1,0:T(8,128)(2,1)} %bitcast.306), channel_id=1, source_target_pairs={{32,0},{64,32},{96,64},{0,96},{33,1},{65,33},{97,65},{1,97},{34,2}... | collective-permute-start | bytes 589832 | tf_op jit(solution)/shard_map/ppermute | solution.py:170
  470.2 39.9 %collective-permute-start.6 = (bf16[64,1536]{1,0:T(8,128)(2,1)}, bf16[64,1536]{1,0:T(8,128)(2,1)}, u32[]{:S(2)}, u32[]{:S(2)}) collective-permute-start(bf16[64,1536]{1,0:T(8,128)(2,1)} %bitcast.305), channel_id=1, source_target_pairs={{0,32},{32,64},{64,96},{96,0},{1,33},{33,65},{65,97},{97,1},{2,34}... | collective-permute-start | bytes 589832 | tf_op jit(solution)/shard_map/ppermute | solution.py:168
  504.4 8.3 collective-permute-start.10
  507.3 12.9 %collective-permute-start.8 = (bf16[64,1536]{1,0:T(8,128)(2,1)}, bf16[64,1536]{1,0:T(8,128)(2,1)}, u32[]{:S(2)}, u32[]{:S(2)}) collective-permute-start(bf16[64,1536]{1,0:T(8,128)(2,1)} %bitcast.305), channel_id=1, source_target_pairs={{32,0},{64,32},{96,64},{0,96},{33,1},{65,33},{97,65},{1,97},{34,2}... | collective-permute-start | bytes 589832 | tf_op jit(solution)/shard_map/ppermute | solution.py:170
  510.2 7.5 collective-permute-start.4
  510.2 11.7 %collective-permute-start.7 = (bf16[64,1536]{1,0:T(8,128)(2,1)}, bf16[64,1536]{1,0:T(8,128)(2,1)}, u32[]{:S(2)}, u32[]{:S(2)}) collective-permute-start(bf16[64,1536]{1,0:T(8,128)(2,1)} %collective-permute-done.6), channel_id=1, source_target_pairs={{0,32},{32,64},{64,96},{96,0},{1,33},{33,65},{65,97},{97,1},{2,34}... | collective-permute-start | bytes 589832 | tf_op jit(solution)/shard_map/ppermute | solution.py:168
  546.3 310.5 %all-reduce.26.cloned.1.call-start = ((), (), s32[]{:S(2)}) async-start(), calls=%async_computation.3 | async-start | bytes 12582912 | tf_op jit(solution)/shard_map/psum | solution.py:188
  561.6 295.1 %copy-start.30 = (bf16[4,64,256]{2,0,1:T(4,128)(2,1)S(1)}, bf16[4,64,256]{2,0,1:T(4,128)(2,1)}, u32[]{:S(2)}) copy-start(bf16[4,64,256]{2,0,1:T(4,128)(2,1)} %copy-done.29) | copy-start | bytes 393220
  561.7 406.3 %all-reduce.30.cloned.1.call-start = ((), (), s32[]{:S(2)}) async-start(), calls=%async_computation.5 | async-start | bytes 1179648
  563.2 295.2 %copy-start.45 = (f32[64,2,6,2]{2,3,1,0:T(2,128)}, f32[64,2,6,2]{2,3,1,0:T(2,128)S(1)}, u32[]{:S(2)}) copy-start(f32[64,2,6,2]{2,3,1,0:T(2,128)S(1)} %get-tuple-element.230) | copy-start | bytes 18436
  865.3 285.1 %all-reduce.28.cloned.1.call-start = ((), (), s32[]{:S(2)}) async-start(), calls=%async_computation.4 | async-start | bytes 1572864
  (58 other events, 533.9 us)
Sparse Core Ops, SparseCore 0:
  106.4 147.3 all-reduce.19
  258.1 98.6 all-reduce.21
  546.4 148.4 all-reduce.23
  700.0 156.7 all-reduce.25
  865.4 102.4 all-reduce.29
  1047.9 102.4 all-reduce.27
